TPU v7x, 256 devices: a whole 4x4x8 slice. The times are simulated.
256 devices in a mesh: section: 4 (over y), dp: 64 (over x, z, core).
Axes of the slice: x: 4, y: 4, z: 8, core: 2. Of those that a mesh axis runs over, the one named last changes fastest.
Arguments:
- hidden_in: bfloat16 [2, 4, 4, 1024, 4096], P(None, 'section', None, 'dp'), may hold values from -6 to 6
- out_grad: bfloat16 [4, 1024, 4096], P(None, 'dp'), may hold values from -6 to 6
- gate_probs: float32 [2, 4, 4, 1024, 2], P(None, 'section', None, 'dp'), may hold values from 0.1 to 1
- expert_ids: int32 [2, 4, 4, 1024, 2], P(None, 'section', None, 'dp'), may hold values from 0 to 7, all different within a row
- task_ids: int32 [4, 64], P(None, 'dp'), may hold values from 0 to 1
- task_embed: float32 [2, 256], replicated, may hold values from -5 to 5
- slot_embed: float32 [2, 4, 8, 256], P(None, 'section'), may hold values from -5 to 5
- gen_down: bfloat16 [256, 65536], P(None, 'dp'), may hold values from -0.0078125 to 0.0078125
- gen_up: bfloat16 [256, 65536], P(None, 'dp'), may hold values from -0.09375 to 0.09375
Outputs:
- d_hidden: bfloat16 [4, 4, 1024, 4096], P('section', None, 'dp')
- d_gen_down: float32 [256, 65536], P(None, 'dp')
- d_gen_up: float32 [256, 65536], P(None, 'dp')
- d_task_embed: float32 [2, 256], replicated
- d_slot_embed: float32 [2, 4, 8, 256], P(None, 'section')
Inputs may be any that keep to these rules, and one draw needn't show every extreme that they name: `expert_ids`: the two experts of a token differ.
All inputs are finite; a program needn't handle non-finite values.
Results may differ from a plain program's by a relative error of at most 0.025.
Values may be sent and summed in bfloat16 or wider, within the bound.
No kernel may reach another device: no remote copies, remote signals or barrier semaphores. Data moves between devices by JAX's collectives and lax.ppermute only.
A program may use at most 64 MiB of HBM per device.

v0:
```python
import jax
import jax.numpy as jnp
from jax import lax
from jax.sharding import PartitionSpec as P

eps = 1e-05


def in_one_piece(arrays, axis, dim, along):
    widths = [a.shape[along] for a in arrays]
    both = jnp.concatenate(arrays, axis=along)
    filled = lax.all_gather(both, axis, axis=dim, tiled=True)
    return tuple(jnp.split(filled, [sum(widths[:k]) for k in range(1, len(widths))], axis=along))


def passed_along(shard, axis, by):
    count = lax.axis_size(axis)
    return lax.ppermute(shard, axis, [(i, (i + by) % count) for i in range(count)])


def sent_together(arrays, axis, dim, along):
    ends, at = ([], 0)
    for a in arrays[:-1]:
        at += a.shape[along]
        ends.append(at)
    both = jnp.concatenate(arrays, axis=along)
    return tuple(
        jnp.split(lax.psum_scatter(both, axis, scatter_dimension=dim, tiled=True), ends, axis=along)
    )


def copy_for_each(shard, axis):
    count = lax.axis_size(axis)
    return lax.all_to_all(
        jnp.broadcast_to(shard[None], (count, *shard.shape)), axis, 0, 0, tiled=True
    )


def taken_together(shard, axis):
    everything = copy_for_each(shard, axis)
    return jnp.sum(everything, axis=0)


def column_weights(gates, choices_ids, task_hot, experts, rank):
    expert_hot = (choices_ids[:, :, None] == jnp.arange(experts, dtype=jnp.int32)).astype(
        jnp.float32
    )
    per_expert = jnp.sum(gates[:, :, None] * expert_hot, axis=1)
    table = task_hot[:, :, None] * per_expert[:, None, :]
    return jnp.repeat(table.reshape(table.shape[0], -1), rank, axis=1)


def layer_back(saved, cot_in, adapt_a, adapt_b, columns):
    values = saved.astype(jnp.float32)
    inv_rms = lax.rsqrt(jnp.mean(values * values, axis=-1, keepdims=True) + eps)
    normed_f = values * inv_rms
    normed = normed_f.astype(jnp.bfloat16)
    contract = (((1,), (1,)), ((), ()))
    low = lax.dot_general(normed, adapt_a, contract, preferred_element_type=jnp.float32)
    mixed_low = (columns * low).astype(jnp.bfloat16)
    back_low = lax.dot_general(cot_in, adapt_b, contract, preferred_element_type=jnp.float32)
    grad_low = (columns * back_low).astype(jnp.bfloat16)
    grad_norm = jnp.dot(grad_low, adapt_a, preferred_element_type=jnp.float32)
    grad_in = inv_rms * (
        grad_norm - normed_f * jnp.mean(grad_norm * normed_f, axis=-1, keepdims=True)
    )
    result = (cot_in.astype(jnp.float32) + grad_in).astype(jnp.bfloat16)
    return (result, normed, mixed_low, grad_low)


def keep_where(active, buffer, block_id, micro_id, fresh):
    return buffer.at[block_id, micro_id].set(jnp.where(active, fresh, buffer[block_id, micro_id]))


def on_device(
    hidden_in, out_grad, gate_probs, expert_ids, task_ids, task_embed, slot_embed, gen_down, gen_up
):
    high = lax.Precision.HIGHEST
    sections = lax.axis_size("section")
    section_id = lax.axis_index("section")
    blocks, _, micro_count, tok_rows, model_width = hidden_in.shape
    task_count, cond_width = task_embed.shape
    experts = slot_embed.shape[2]
    combos = task_count * experts
    pre_act = task_embed[None, :, None, :] + slot_embed[:, 0][:, None, :, :]
    conditions = jax.nn.silu(pre_act).reshape(blocks, combos, cond_width)
    gen_down_f = gen_down.astype(jnp.float32)
    gen_up_f = gen_up.astype(jnp.float32)
    shard_a = jnp.einsum("jcw,wf->jcf", conditions, gen_down_f, precision=high).astype(jnp.bfloat16)
    shard_b = jnp.einsum("jcw,wf->jcf", conditions, gen_up_f, precision=high).astype(jnp.bfloat16)
    full_a, full_b = in_one_piece((shard_a, shard_b), "dp", 2, 0)
    adapt_a = full_a.reshape(blocks, -1, model_width)
    adapt_b = full_b.reshape(blocks, -1, model_width)
    ranks_all = adapt_a.shape[1]
    rank = ranks_all // combos
    total_items = blocks * micro_count

    def tick(tick_no, carry):
        incoming, normed_buf, cot_buf, low_buf, grad_low_buf, hidden_out = carry
        position = tick_no - (sections - 1 - section_id)
        active = (position >= 0) & (position < total_items)
        clipped = jnp.clip(position, 0, total_items - 1)
        block_id = blocks - 1 - clipped // micro_count
        micro_id = clipped % micro_count
        fresh_start = (section_id == sections - 1) & (clipped < micro_count)
        cot_in = jnp.where(fresh_start, out_grad[micro_id], incoming)
        task_hot = jnp.broadcast_to(
            (jnp.arange(task_count, dtype=jnp.int32) == task_ids[micro_id, 0]).astype(jnp.float32),
            (tok_rows, task_count),
        )
        columns = column_weights(
            gate_probs[block_id, 0, micro_id],
            expert_ids[block_id, 0, micro_id],
            task_hot,
            experts,
            rank,
        )
        result, normed, mixed_low, grad_low = layer_back(
            hidden_in[block_id, 0, micro_id], cot_in, adapt_a[block_id], adapt_b[block_id], columns
        )
        normed_buf = keep_where(active, normed_buf, block_id, micro_id, normed)
        cot_buf = keep_where(active, cot_buf, block_id, micro_id, cot_in)
        low_buf = keep_where(active, low_buf, block_id, micro_id, mixed_low)
        grad_low_buf = keep_where(active, grad_low_buf, block_id, micro_id, grad_low)
        hidden_out = hidden_out.at[micro_id].set(
            jnp.where(active & (block_id == 0), result, hidden_out[micro_id])
        )
        outgoing = passed_along(result, "section", -1)
        return (outgoing, normed_buf, cot_buf, low_buf, grad_low_buf, hidden_out)

    carry = (
        jnp.zeros((tok_rows, model_width), jnp.bfloat16),
        jnp.zeros((blocks, micro_count, tok_rows, model_width), jnp.bfloat16),
        jnp.zeros((blocks, micro_count, tok_rows, model_width), jnp.bfloat16),
        jnp.zeros((blocks, micro_count, tok_rows, ranks_all), jnp.bfloat16),
        jnp.zeros((blocks, micro_count, tok_rows, ranks_all), jnp.bfloat16),
        jnp.zeros((micro_count, tok_rows, model_width), jnp.bfloat16),
    )
    rows_contract = (((0,), (0,)), ((), ()))

    def block_grads(state, block_id):
        normed_all = state[1][block_id].reshape(-1, model_width)
        cot_all = state[2][block_id].reshape(-1, model_width)
        low_all = state[3][block_id].reshape(-1, ranks_all)
        grad_low_all = state[4][block_id].reshape(-1, ranks_all)
        grad_a = lax.dot_general(
            grad_low_all, normed_all, rows_contract, preferred_element_type=jnp.float32
        )
        grad_b = lax.dot_general(
            low_all, cot_all, rows_contract, preferred_element_type=jnp.float32
        )
        return (grad_a.reshape(combos, -1), grad_b.reshape(combos, -1))

    carry = lax.fori_loop(0, total_items + sections - 1, tick, carry)
    pairs = [block_grads(carry, block_id) for block_id in range(blocks)]
    stack_a = jnp.stack([pair[0] for pair in pairs])
    stack_b = jnp.stack([pair[1] for pair in pairs])
    reduced_a, reduced_b = tuple(
        (
            part.astype(jnp.float32)
            for part in sent_together(
                (stack_a.astype(jnp.bfloat16), stack_b.astype(jnp.bfloat16)), "dp", 2, 0
            )
        )
    )
    hidden_out = carry[5]
    grad_scale = 1.0 / (micro_count * tok_rows * lax.axis_size("dp"))
    reduced_a = reduced_a * grad_scale
    reduced_b = reduced_b * grad_scale
    part_down = jnp.einsum("jcw,jcf->wf", conditions, reduced_a, precision=high)
    part_up = jnp.einsum("jcw,jcf->wf", conditions, reduced_b, precision=high)
    d_gen_down, d_gen_up = (
        lax.psum(part_down.astype(jnp.bfloat16), "section").astype(jnp.float32),
        lax.psum(part_up.astype(jnp.bfloat16), "section").astype(jnp.float32),
    )
    d_cond = jnp.einsum("jcf,wf->jcw", reduced_a, gen_down_f, precision=high)
    d_cond = d_cond + jnp.einsum("jcf,wf->jcw", reduced_b, gen_up_f, precision=high)
    sigmoid_pre = jax.nn.sigmoid(pre_act)
    d_pre = d_cond.reshape(pre_act.shape) * sigmoid_pre * (1.0 + pre_act * (1.0 - sigmoid_pre))
    d_pre_sum = taken_together(d_pre, "dp")
    d_slot = jnp.sum(d_pre_sum, axis=1)
    d_task = taken_together(jnp.sum(d_pre_sum, axis=(0, 2)), "section")
    return (hidden_out[None], d_gen_down, d_gen_up, d_task, d_slot[:, None])


def solution(mesh):
    placed = (
        P(None, "section", None, "dp", None),
        P(None, "dp", None),
        P(None, "section", None, "dp", None),
        P(None, "section", None, "dp", None),
        P(None, "dp"),
        P(),
        P(None, "section", None, None),
        P(None, "dp"),
        P(None, "dp"),
    )
    return jax.shard_map(
        on_device,
        mesh=mesh,
        in_specs=placed,
        out_specs=(
            P("section", None, "dp", None),
            P(None, "dp"),
            P(None, "dp"),
            P(),
            P(None, "section", None, None),
        ),
        check_vma=False,
    )
```

profile of v0, /device:TPU:1, one launch (start us, length us, event | category | flops | bytes accessed | tf_op | source)
XLA Modules:
  0.0 647.0 jit_solution(1743381916473888109)
XLA Ops:
  11.2 87.3 %all-gather.2.cloned.1.call-done = bf16[4,16,65536]{2,1,0:T(8,128)(2,1)} async-done(((bf16[4,16,1024]{2,1,0:T(8,128)(2,1)}), bf16[4,16,65536]{2,1,0:T(8,128)(2,1)}) %all-gather.2.cloned.1.call-update) | async-done | bytes 8388624 | tf_op jit(solution)/shard_map/all_gather | solution.py:12
  98.6 5.7 fusion.116
  104.3 5.6 reshape.497
  109.9 5.7 reshape.496
  118.1 269.2 %while.30 = (s32[]{:T(128)}, bf16[16,4096]{1,0:T(8,128)(2,1)S(1)}, bf16[2,4,16,4096]{3,2,1,0:T(8,128)(2,1)}, bf16[2,4,16,4096]{3,2,1,0:T(8,128)(2,1)S(1)}, bf16[...) while((s32[]{:T(128)}, bf16[16,4096]{1,0:T(8,128)(2,1)S(1)}, ...), condition=%wide.region_6.7_spmd, body=%wide.region_0.6_spmd.sunk | while | flops 102532064 | bytes 10274659 | solution.py:154
  140.6 3.6 fusion.144
  164.7 3.6 fusion.144
  188.5 3.6 fusion.144
  212.3 3.6 fusion.144
  238.2 3.6 fusion.144
  262.3 3.6 fusion.144
  276.3 3.5 fusion.140
  286.1 3.6 fusion.144
  309.9 3.6 fusion.144
  335.9 3.6 fusion.144
  349.8 3.5 fusion.140
  360.0 3.6 fusion.144
  373.9 3.5 fusion.140
  383.8 3.6 fusion.144
  409.4 6.6 %pad_maximum_fusion = bf16[4,16,65536]{2,1,0:T(8,128)(2,1)} fusion(bf16[1,16,65536]{2,1,0:T(8,128)(2,1)} %stack_reshape.19, bf16[1,16,65536]{2,1,0:T(8,128)(2,1)} %stack_reshape.18, bf16[1,16,65536]{2,1,0:T(8,128)(2,1)} %stack_reshape.17, bf16[1,16,65536]{2,1,0:T(8,128)(2,1)S(1)} %stack_reshape.16), kind=kLoop, calls=%fused_computation.68 | loop fusion | flops 12582912 | bytes 16777216 | tf_op jit(solution)/shard_map/concatenate | solution.py:26
  416.1 146.1 %reduce-scatter.2.cloned.1.call-done = bf16[4,16,1024]{2,1,0:T(8,128)(2,1)} async-done(((bf16[4,16,65536]{2,1,0:T(8,128)(2,1)}), bf16[4,16,1024]{2,1,0:T(8,128)(2,1)}) %reduce-scatter.2.cloned.1.call-update) | async-done | bytes 131088 | tf_op jit(solution)/shard_map/reduce_scatter | solution.py:28
  566.6 12.4 %all-to-all-start = ((f32[64,2,2,8,256]{4,3,2,1,0:T(8,128)}), f32[64,2,2,8,256]{4,3,2,1,0:T(8,128)S(1)}, u32[]{:S(2)}, u32[]{:S(2)}) async-start(f32[64,2,2,8,256]{4,3,2,1,0:T(8,128)} %broadcast_in_dim.76), calls=%async_computation.1 | async-start | bytes 4194304 | tf_op jit(solution)/shard_map/all_to_all | solution.py:34
  582.8 47.5 %all-to-all-done = f32[64,2,2,8,256]{4,3,2,1,0:T(8,128)S(1)} async-done(((f32[64,2,2,8,256]{4,3,2,1,0:T(8,128)}), f32[64,2,2,8,256]{4,3,2,1,0:T(8,128)S(1)}, u32[]{:S(2)}, u32[]{:S(2)}) %all-to-all-start) | async-done | bytes 2097184 | tf_op jit(solution)/shard_map/all_to_all | solution.py:34
  631.7 4.0 all-to-all-start.1
  (374 shorter events, 261.5 us)
Async XLA Ops:
  7.2 91.4 %all-gather.2.cloned.1.call-start = ((), (), s32[]{:S(2)}) async-start(), calls=%async_computation.3 | async-start | bytes 8519680 | tf_op jit(solution)/shard_map/all_gather | solution.py:12
  11.2 550.9 %reduce-scatter.2.cloned.1.call-start = ((), (), s32[]{:S(2)}) async-start(), calls=%async_computation.4 | async-start | bytes 8519680 | tf_op jit(solution)/shard_map/reduce_scatter | solution.py:28
  135.0 9.2 %collective-permute-start = (bf16[16,4096]{1,0:T(8,128)(2,1)S(1)}, bf16[16,4096]{1,0:T(8,128)(2,1)S(1)}, u32[]{:S(2)}, u32[]{:S(2)}) collective-permute-start(bf16[16,4096]{1,0:T(8,128)(2,1)S(1)} %get-tuple-element.652), channel_id=1, source_target_pairs={{0,192},{64,0},{128,64},{192,128},{1,193},{65,1},{129,65},{193,129... | collective-permute-start | bytes 393224 | tf_op jit(solution)/shard_map/while/body/eval_jaxpr/ppermute | solution.py:18
  161.0 7.3 %collective-permute-start = (bf16[16,4096]{1,0:T(8,128)(2,1)S(1)}, bf16[16,4096]{1,0:T(8,128)(2,1)S(1)}, u32[]{:S(2)}, u32[]{:S(2)}) collective-permute-start(bf16[16,4096]{1,0:T(8,128)(2,1)S(1)} %get-tuple-element.652), channel_id=1, source_target_pairs={{0,192},{64,0},{128,64},{192,128},{1,193},{65,1},{129,65},{193,129... | collective-permute-start | bytes 393224 | tf_op jit(solution)/shard_map/while/body/eval_jaxpr/ppermute | solution.py:18
  185.0 7.0 %collective-permute-start = (bf16[16,4096]{1,0:T(8,128)(2,1)S(1)}, bf16[16,4096]{1,0:T(8,128)(2,1)S(1)}, u32[]{:S(2)}, u32[]{:S(2)}) collective-permute-start(bf16[16,4096]{1,0:T(8,128)(2,1)S(1)} %get-tuple-element.652), channel_id=1, source_target_pairs={{0,192},{64,0},{128,64},{192,128},{1,193},{65,1},{129,65},{193,129... | collective-permute-start | bytes 393224 | tf_op jit(solution)/shard_map/while/body/eval_jaxpr/ppermute | solution.py:18
  208.8 7.0 %collective-permute-start = (bf16[16,4096]{1,0:T(8,128)(2,1)S(1)}, bf16[16,4096]{1,0:T(8,128)(2,1)S(1)}, u32[]{:S(2)}, u32[]{:S(2)}) collective-permute-start(bf16[16,4096]{1,0:T(8,128)(2,1)S(1)} %get-tuple-element.652), channel_id=1, source_target_pairs={{0,192},{64,0},{128,64},{192,128},{1,193},{65,1},{129,65},{193,129... | collective-permute-start | bytes 393224 | tf_op jit(solution)/shard_map/while/body/eval_jaxpr/ppermute | solution.py:18
  221.6 10.2 %copy-start.9 = (f32[16]{0:T(128)S(1)}, f32[16]{0:T(128)}, u32[]{:S(2)}) copy-start(f32[16]{0:T(128)} %add_rsqrt_fusion.2) | copy-start | bytes 196 | tf_op jit(solution)/shard_map/while
  232.6 9.2 %collective-permute-start = (bf16[16,4096]{1,0:T(8,128)(2,1)S(1)}, bf16[16,4096]{1,0:T(8,128)(2,1)S(1)}, u32[]{:S(2)}, u32[]{:S(2)}) collective-permute-start(bf16[16,4096]{1,0:T(8,128)(2,1)S(1)} %get-tuple-element.652), channel_id=1, source_target_pairs={{0,192},{64,0},{128,64},{192,128},{1,193},{65,1},{129,65},{193,129... | collective-permute-start | bytes 393224 | tf_op jit(solution)/shard_map/while/body/eval_jaxpr/ppermute | solution.py:18
  258.6 7.3 %collective-permute-start = (bf16[16,4096]{1,0:T(8,128)(2,1)S(1)}, bf16[16,4096]{1,0:T(8,128)(2,1)S(1)}, u32[]{:S(2)}, u32[]{:S(2)}) collective-permute-start(bf16[16,4096]{1,0:T(8,128)(2,1)S(1)} %get-tuple-element.652), channel_id=1, source_target_pairs={{0,192},{64,0},{128,64},{192,128},{1,193},{65,1},{129,65},{193,129... | collective-permute-start | bytes 393224 | tf_op jit(solution)/shard_map/while/body/eval_jaxpr/ppermute | solution.py:18
  282.7 7.0 %collective-permute-start = (bf16[16,4096]{1,0:T(8,128)(2,1)S(1)}, bf16[16,4096]{1,0:T(8,128)(2,1)S(1)}, u32[]{:S(2)}, u32[]{:S(2)}) collective-permute-start(bf16[16,4096]{1,0:T(8,128)(2,1)S(1)} %get-tuple-element.652), channel_id=1, source_target_pairs={{0,192},{64,0},{128,64},{192,128},{1,193},{65,1},{129,65},{193,129... | collective-permute-start | bytes 393224 | tf_op jit(solution)/shard_map/while/body/eval_jaxpr/ppermute | solution.py:18
  306.5 7.0 %collective-permute-start = (bf16[16,4096]{1,0:T(8,128)(2,1)S(1)}, bf16[16,4096]{1,0:T(8,128)(2,1)S(1)}, u32[]{:S(2)}, u32[]{:S(2)}) collective-permute-start(bf16[16,4096]{1,0:T(8,128)(2,1)S(1)} %get-tuple-element.652), channel_id=1, source_target_pairs={{0,192},{64,0},{128,64},{192,128},{1,193},{65,1},{129,65},{193,129... | collective-permute-start | bytes 393224 | tf_op jit(solution)/shard_map/while/body/eval_jaxpr/ppermute | solution.py:18
  330.3 9.2 %collective-permute-start = (bf16[16,4096]{1,0:T(8,128)(2,1)S(1)}, bf16[16,4096]{1,0:T(8,128)(2,1)S(1)}, u32[]{:S(2)}, u32[]{:S(2)}) collective-permute-start(bf16[16,4096]{1,0:T(8,128)(2,1)S(1)} %get-tuple-element.652), channel_id=1, source_target_pairs={{0,192},{64,0},{128,64},{192,128},{1,193},{65,1},{129,65},{193,129... | collective-permute-start | bytes 393224 | tf_op jit(solution)/shard_map/while/body/eval_jaxpr/ppermute | solution.py:18
  345.3 10.2 %copy-start.9 = (f32[16]{0:T(128)S(1)}, f32[16]{0:T(128)}, u32[]{:S(2)}) copy-start(f32[16]{0:T(128)} %add_rsqrt_fusion.2) | copy-start | bytes 196 | tf_op jit(solution)/shard_map/while
  356.3 7.3 %collective-permute-start = (bf16[16,4096]{1,0:T(8,128)(2,1)S(1)}, bf16[16,4096]{1,0:T(8,128)(2,1)S(1)}, u32[]{:S(2)}, u32[]{:S(2)}) collective-permute-start(bf16[16,4096]{1,0:T(8,128)(2,1)S(1)} %get-tuple-element.652), channel_id=1, source_target_pairs={{0,192},{64,0},{128,64},{192,128},{1,193},{65,1},{129,65},{193,129... | collective-permute-start | bytes 393224 | tf_op jit(solution)/shard_map/while/body/eval_jaxpr/ppermute | solution.py:18
  369.4 10.2 %copy-start.9 = (f32[16]{0:T(128)S(1)}, f32[16]{0:T(128)}, u32[]{:S(2)}) copy-start(f32[16]{0:T(128)} %add_rsqrt_fusion.2) | copy-start | bytes 196 | tf_op jit(solution)/shard_map/while
  380.4 7.0 %collective-permute-start = (bf16[16,4096]{1,0:T(8,128)(2,1)S(1)}, bf16[16,4096]{1,0:T(8,128)(2,1)S(1)}, u32[]{:S(2)}, u32[]{:S(2)}) collective-permute-start(bf16[16,4096]{1,0:T(8,128)(2,1)S(1)} %get-tuple-element.652), channel_id=1, source_target_pairs={{0,192},{64,0},{128,64},{192,128},{1,193},{65,1},{129,65},{193,129... | collective-permute-start | bytes 393224 | tf_op jit(solution)/shard_map/while/body/eval_jaxpr/ppermute | solution.py:18
  416.0 147.6 %copy-start.4 = (bf16[256,1024]{1,0:T(8,128)(2,1)S(1)}, bf16[256,1024]{1,0:T(8,128)(2,1)}, u32[]{:S(2)}) copy-start(bf16[256,1024]{1,0:T(8,128)(2,1)} %param.29) | copy-start | bytes 1572868
  416.0 147.6 %copy-start.8 = (f32[2,1,8,256]{3,2,1,0:T(8,128)S(1)}, f32[2,1,8,256]{3,2,1,0:T(8,128)}, u32[]{:S(2)}) copy-start(f32[2,1,8,256]{3,2,1,0:T(8,128)} %param.27) | copy-start | bytes 49156
  416.0 147.6 %copy-start.11 = (f32[2,256]{1,0:T(2,128)S(1)}, f32[2,256]{1,0:T(2,128)}, u32[]{:S(2)}) copy-start(f32[2,256]{1,0:T(2,128)} %param.26) | copy-start | bytes 6148
  416.1 163.0 %copy-start.7 = (f32[16,256]{1,0:T(8,128)S(1)}, f32[16,256]{1,0:T(8,128)}, u32[]{:S(2)}) copy-start(f32[16,256]{1,0:T(8,128)} %copy-done.6) | copy-start | bytes 49156
  562.1 16.9 %copy-start.5 = (bf16[4,16,1024]{2,1,0:T(8,128)(2,1)S(1)}, bf16[4,16,1024]{2,1,0:T(8,128)(2,1)}, u32[]{:S(2)}) copy-start(bf16[4,16,1024]{2,1,0:T(8,128)(2,1)} %reduce-scatter.2.cloned.1.call-done) | copy-start | bytes 393220
  566.6 63.6 %all-to-all-start = ((f32[64,2,2,8,256]{4,3,2,1,0:T(8,128)}), f32[64,2,2,8,256]{4,3,2,1,0:T(8,128)S(1)}, u32[]{:S(2)}, u32[]{:S(2)}) async-start(f32[64,2,2,8,256]{4,3,2,1,0:T(8,128)} %broadcast_in_dim.76), calls=%async_computation.1 | async-start | bytes 4194304 | tf_op jit(solution)/shard_map/all_to_all | solution.py:34
  579.0 56.6 %all-reduce.3.cloned.1.call-start = ((), (), s32[]{:S(2)}) async-start(), calls=%async_computation.5 | async-start | bytes 2097152 | tf_op jit(solution)/shard_map/psum | solution.py:173
  631.7 8.2 %all-to-all-start.1 = ((f32[4,2,256]{2,1,0:T(2,128)}), f32[4,2,256]{2,1,0:T(2,128)S(1)}, u32[]{:S(2)}, u32[]{:S(2)}) async-start(f32[4,2,256]{2,1,0:T(2,128)} %broadcast_in_dim.77), calls=%async_computation.2 | async-start | bytes 16384 | tf_op jit(solution)/shard_map/all_to_all | solution.py:34
  (14 other events, 105.9 us)
Sparse Core Ops, SparseCore 0:
  11.4 87.1 all-gather.1
  416.2 145.9 reduce-scatter.1
  583.0 50.9 all-reduce.2
where the time goes:
time: 652 us; the launch traced here: 647 us
  waiting for transfers between devices  281 us (43%)
  matrix products  120 us (18%)
  other arithmetic  113 us (17%)
  local copies, waits for them, and re-layouts  89.9 us (14%)
  starting transfers between devices  27.7 us (4%)
  between operations  13.9 us (2%)
    reduce_scatter x1, waiting for transfers between devices, sent_together(): lax.psum_scatter(both, axis, scatter_dimension=dim, tiled=True)  146 us
    all_gather x1, waiting for transfers between devices, in_one_piece(): filled = lax.all_gather(both, axis, axis=dim, tiled=True)  87.3 us
    all_to_all x2, waiting for transfers between devices, copy_for_each(): lax.all_to_all(jnp.broadcast_to(shard[None], (count, *shard.shape)), axis...  47.5 us
    scatter x22, other arithmetic, keep_where(): buffer.at[block_id, micro_id]  44.4 us
    dot_general x11, matrix products, layer_back(): lax.dot_general(normed, adapt_a, contract, preferred_element_type=jnp.flo...  39.1 us
    dot_general x11, matrix products, layer_back(): lax.dot_general(cot_in, adapt_b, contract, preferred_element_type=jnp.flo...  39 us
    another operation x22, other arithmetic  31.7 us
    dot_general x11, matrix products, layer_back(): grad_norm = jnp.dot(grad_low, adapt_a, preferred_element_type=jnp.float32)  23 us
  transfers between devices with their start and end apart: 16, of which 3 were waited for; matrix products, arithmetic and copies ran while one was open for 13% of the time, Pallas kernels for 0%

commit v1 on v0

v1 whole, which is shorter than its diff:
```python
import functools

import jax
import jax.numpy as jnp
from jax import lax
from jax.experimental import pallas as pl
from jax.experimental.pallas import tpu as pltpu
from jax.sharding import Mesh, PartitionSpec as P

eps = 1e-05
bf16 = jnp.bfloat16
f32 = jnp.float32

AXES = ("s", "x", "zh", "zl", "c")
DP = ("x", "zh", "zl", "c")
RANKS = ("x", "zh")
QUARTERS = ("zl", "c")
VMEM = pl.BlockSpec(memory_space=pltpu.VMEM)
SMEM = pl.BlockSpec(memory_space=pltpu.SMEM)
LAST = (((1,), (1,)), ((), ()))
FIRST = (((0,), (0,)), ((), ()))


def adapter_rows(g_ref, block, which, q):
    part = g_ref[:, q, block, which]
    return part.reshape(part.shape[0] * part.shape[1], part.shape[2])


def low_kernel(xn_ref, weights_ref, g_ref, out_ref):
    blocks = out_ref.shape[0]
    quarters, width = g_ref.shape[1], g_ref.shape[5]
    for j in range(blocks):
        low = jnp.zeros(out_ref.shape[1:], f32)
        for q in range(quarters):
            low += lax.dot_general(
                xn_ref[j, :, q * width : (q + 1) * width],
                adapter_rows(g_ref, j, 0, q),
                LAST,
                preferred_element_type=f32,
            )
        out_ref[j] = (weights_ref[j] * low).astype(bf16)


def tick_kernel(first, where_ref, *refs):
    if first:
        grad_ref, x_ref, inv_ref, weights_ref, g_ref, dx_ref, du_ref, cot_ref = refs
        cot_ref[...] = grad_ref[...]
    else:
        in_ref, x_ref, inv_ref, weights_ref, g_ref, dx_ref, du_ref = refs
        cot_ref = in_ref
    block, item = where_ref[0], where_ref[1]
    quarters, width = g_ref.shape[1], g_ref.shape[5]
    back = jnp.zeros(du_ref.shape, f32)
    for q in range(quarters):
        back += lax.dot_general(
            cot_ref[:, q * width : (q + 1) * width],
            adapter_rows(g_ref, block, 1, q),
            LAST,
            preferred_element_type=f32,
        )
    du = (weights_ref[item] * back).astype(bf16)
    du_ref[...] = du
    inv = inv_ref[item][:, :1]
    dxn, xf = [], []
    total = jnp.zeros((du.shape[0], 1), f32)
    for q in range(quarters):
        xf.append(x_ref[item, :, q * width : (q + 1) * width].astype(f32) * inv)
        dxn.append(
            jnp.dot(du, adapter_rows(g_ref, block, 0, q), preferred_element_type=f32)
        )
        total += jnp.sum(dxn[q] * xf[q], axis=1, keepdims=True)
    mean = total * (1.0 / (quarters * width))
    for q in range(quarters):
        cols = slice(q * width, (q + 1) * width)
        dx_ref[:, cols] = (
            cot_ref[:, cols].astype(f32) + inv * (dxn[q] - xf[q] * mean)
        ).astype(bf16)


def grads_kernel(mixed_ref, xn_ref, out_ref):
    width = xn_ref.shape[1]
    ranks, rows = out_ref.shape[0], out_ref.shape[1] // 2
    high = ranks * rows
    dy = mixed_ref[:, :width]
    du = mixed_ref[:, width : width + high]
    low = mixed_ref[:, width + high :]
    grad_a = lax.dot_general(du, xn_ref[...], FIRST, preferred_element_type=f32)
    out_ref[:, :rows, :] = grad_a.astype(bf16).reshape(ranks, rows, width)
    grad_b = lax.dot_general(low, dy, FIRST, preferred_element_type=f32)
    out_ref[:, rows:, :] = grad_b.astype(bf16).reshape(ranks, rows, width)


def call(kernel, out_shape, scalars, operands, flops, moved):
    return pl.pallas_call(
        kernel,
        out_shape=out_shape,
        in_specs=[SMEM] * scalars + [VMEM] * (len(operands) - scalars),
        out_specs=jax.tree.map(lambda _: VMEM, out_shape),
        compiler_params=pltpu.CompilerParams(vmem_limit_bytes=32 * 1024 * 1024),
        cost_estimate=pl.CostEstimate(flops=flops, bytes_accessed=moved, transcendentals=0),
    )(*operands)


def summed_over(part, axes):
    for axis in axes:
        part = jnp.sum(lax.all_gather(part, axis), axis=0)
    return part


def on_device(
    hidden_in, out_grad, gate_probs, expert_ids, task_ids, task_embed, slot_embed, gen_down, gen_up
):
    high = lax.Precision.HIGHEST
    sections = lax.axis_size("s")
    section_id = lax.axis_index("s")
    quarters = lax.axis_size(QUARTERS)
    ranks = lax.axis_size(RANKS)
    blocks, _, micros, rows, model = hidden_in.shape
    tasks, cond_width = task_embed.shape
    experts = slot_embed.shape[2]
    combos = tasks * experts
    width = model // quarters
    wide = ranks * combos
    items = blocks * micros
    tokens = micros * rows

    pre = task_embed[None, :, None, :] + slot_embed[:, 0][:, None, :, :]
    cond = jax.nn.silu(pre).reshape(blocks, combos, cond_width)
    gen_a = jnp.einsum("jcw,wf->jcf", cond, gen_down.astype(f32), precision=high).astype(bf16)
    gen_b = jnp.einsum("jcw,wf->jcf", cond, gen_up.astype(f32), precision=high).astype(bf16)
    mine = jnp.stack([gen_a, gen_b], axis=1).reshape(blocks * 2 * combos, width)
    filled = lax.all_gather(mine, DP, axis=0, tiled=True)
    adapters = filled.reshape(ranks, quarters, blocks, 2, combos, width)

    slots = lax.all_gather(slot_embed[:, 0], "s")
    pre_all = task_embed[None, None, :, None, :] + slots[:, :, None, :, :]
    cond_all = jax.nn.silu(pre_all).reshape(sections * blocks * combos, cond_width)
    saved = hidden_in[:, 0]
    values = saved.astype(f32)
    inv = lax.rsqrt(jnp.mean(values * values, axis=-1, keepdims=True) + eps)
    normed = (values * inv).astype(bf16).reshape(blocks, tokens, model)
    inv_items = jnp.broadcast_to(inv, (blocks, micros, rows, 128)).reshape(items, rows, 128)
    x_items = saved.reshape(items, rows, model)
    lane = jnp.arange(wide, dtype=jnp.int32)
    expert_of, task_of = lane % experts, (lane // experts) % tasks
    ids, gates = expert_ids[:, 0], gate_probs[:, 0]
    weights = jnp.where(ids[..., 0:1] == expert_of, gates[..., 0:1], 0.0) + jnp.where(
        ids[..., 1:2] == expert_of, gates[..., 1:2], 0.0
    )
    weights = jnp.where(task_ids[None, :, :, None] == task_of, weights, 0.0)
    weights_items = weights.reshape(items, rows, wide)
    normed_send = normed.reshape(blocks, tokens, quarters, width).transpose(2, 0, 1, 3)
    normed_quarter = lax.all_to_all(normed_send, QUARTERS, 0, 0)

    low = call(
        low_kernel,
        jax.ShapeDtypeStruct((blocks, tokens, wide), bf16),
        0,
        (normed, weights.reshape(blocks, tokens, wide), adapters),
        2 * blocks * tokens * wide * model,
        3 << 21,
    )

    def step(tick, incoming):
        position = jnp.clip(tick - (sections - 1 - section_id), 0, items - 1)
        block = blocks - 1 - position // micros
        item = block * micros + position % micros
        where = jnp.stack([block, item]).astype(jnp.int32)
        operands = (where, incoming, x_items, inv_items, weights_items, adapters)
        outs = call(
            functools.partial(tick_kernel, False),
            (
                jax.ShapeDtypeStruct((rows, model), bf16),
                jax.ShapeDtypeStruct((rows, wide), bf16),
            ),
            1,
            operands,
            4 * rows * wide * model,
            5 << 20,
        )
        return outs

    cots, dus, results = [], [], []
    incoming = jnp.zeros((rows, model), bf16)
    pairs = [(i, (i - 1) % sections) for i in range(sections)]
    reduced = [None] * blocks

    def layer_sum(block):
        start = (blocks - 1 - block) * micros
        def chosen(kept, m):
            return lax.select_n(
                section_id, *[kept[start + m + sections - 1 - s] for s in range(sections)]
            )
        dy = jnp.concatenate([chosen(cots, m) for m in range(micros)])
        du = jnp.concatenate([chosen(dus, m) for m in range(micros)])
        dy = dy.reshape(tokens, quarters, width).transpose(1, 0, 2)
        both = jnp.concatenate([du, low[block]], axis=1)
        both = jnp.broadcast_to(both[None], (quarters, tokens, 2 * wide))
        mixed = lax.all_to_all(jnp.concatenate([dy, both], axis=2), QUARTERS, 0, 0)
        part = call(
            grads_kernel,
            jax.ShapeDtypeStruct((ranks, 2 * combos, width), bf16),
            0,
            (
                mixed.reshape(quarters * tokens, width + 2 * wide),
                normed_quarter[:, block].reshape(quarters * tokens, width),
            ),
            4 * quarters * tokens * wide * width,
            3 << 20,
        )
        got = lax.all_to_all(part, RANKS, 0, 0)
        scale = 1.0 / (micros * rows * lax.axis_size(DP))
        return (jnp.sum(got.astype(f32), axis=0) * scale).astype(bf16)

    for tick in range(items + sections - 1):
        if tick < micros:
            fresh = section_id == sections - 1
            incoming = jnp.where(fresh, out_grad[tick], incoming)
        result, du = step(tick, incoming)
        cots.append(incoming)
        dus.append(du)
        results.append(result)
        if tick < items + sections - 2:
            incoming = lax.ppermute(result, "s", pairs)
        if tick == micros + sections - 2:
            reduced[1] = layer_sum(1)
    reduced[0] = layer_sum(0)

    hidden_out = jnp.stack(
        [
            lax.select_n(
                section_id,
                *[results[micros + m + sections - 1 - s] for s in range(sections)],
            )
            for m in range(micros)
        ]
    )
    all_layers = lax.all_gather(jnp.stack(reduced), "s")
    grads = all_layers.reshape(sections * blocks, 2, combos, width)
    grad_a = grads[:, 0].reshape(-1, width)
    grad_b = grads[:, 1].reshape(-1, width)
    d_cond = jnp.einsum("nf,wf->nw", grad_a, gen_down, preferred_element_type=f32)
    d_cond = d_cond + jnp.einsum("nf,wf->nw", grad_b, gen_up, preferred_element_type=f32)
    gate = jax.nn.sigmoid(pre_all)
    d_pre = d_cond.reshape(pre_all.shape) * gate * (1.0 + pre_all * (1.0 - gate))
    own = lax.dynamic_index_in_dim(d_pre, section_id, 0, keepdims=False)
    d_slot = jnp.sum(own, axis=1).reshape(blocks * experts, cond_width)
    d_task = jnp.sum(d_pre, axis=(0, 1, 3))
    small = summed_over(jnp.concatenate([d_slot, d_task]), (QUARTERS, "x", "zh"))
    d_slot = small[: blocks * experts].reshape(blocks, 1, experts, cond_width)
    d_task = small[blocks * experts :]
    d_gen_down = jnp.einsum("nw,nf->wf", cond_all, grad_a.astype(f32), precision=high)
    d_gen_up = jnp.einsum("nw,nf->wf", cond_all, grad_b.astype(f32), precision=high)
    return (hidden_out[None], d_gen_down, d_gen_up, d_task, d_slot)


def solution(mesh):
    split = Mesh(mesh.devices.reshape(mesh.devices.shape[0], 4, 4, 2, 2), AXES)
    placed = (
        P(None, "s", None, DP, None),
        P(None, DP, None),
        P(None, "s", None, DP, None),
        P(None, "s", None, DP, None),
        P(None, DP),
        P(),
        P(None, "s", None, None),
        P(None, DP),
        P(None, DP),
    )
    return jax.shard_map(
        on_device,
        mesh=split,
        in_specs=placed,
        out_specs=(
            P("s", None, DP, None),
            P(None, DP),
            P(None, DP),
            P(),
            P(None, "s", None, None),
        ),
        check_vma=False,
    )
```

time: 652 us -> 382 us (0.59)
  waiting for transfers between devices: 281 us -> 159 us
  matrix products: 120 us -> 6.27 us
  other arithmetic: 113 us -> 13.2 us
  blocking collectives: 0 us -> 52 us
  local copies, waits for them, and re-layouts: 89.9 us -> 40.8 us
  Pallas kernels: 0 us -> 32 us
  starting transfers between devices: 27.7 us -> 58.7 us
    reduce_scatter x1 -> x0, waiting for transfers between devices: 146 us -> none  [sent_together(): lax.psum_scatter(both, axis, scatter_dimension=dim, tiled=True)]
    dot_general x43 -> x6, matrix products: 120 us -> 6.27 us  [the longest x1 1.59 us: on_device(): jnp.einsum('nw,nf->wf', cond_all, grad_a.astype(f32), precision=high)]
    scatter x33 -> x0, other arithmetic: 53.1 us -> none  [the longest x22 44.4 us: keep_where(): buffer.at[block_id, micro_id]]
    all_gather x0 -> x5, blocking collectives: none -> 52 us  [the longest x3 30.7 us: summed_over(): part = jnp.sum(lax.all_gather(part, axis), axis=0)]
    dynamic_slice x55 -> x0, local copies, waits for them, and re-layouts: 36 us -> none  [the longest x33 22.2 us: keep_where(): buffer[block_id, micro_id]]
    pallas_call x0 -> x14, Pallas kernels: none -> 32 us  [call(): pl.pallas_call(kernel, out_shape=out_shape, in_specs=[SMEM] * scalars + [...]
    unnamed x22 -> x56, local copies, waits for them, and re-layouts: 0.06 us -> 30.5 us
    another operation x22 -> x14, other arithmetic: 31.7 us -> 1.96 us  [the longest x1 1.09 us: on_device(): jnp.stack([lax.select_n(section_id, *[results[micros + m + sections - 1 -...]
  transfers between devices with their start and end apart: 16 -> 16, of which waited for: 3 -> 13; matrix products, arithmetic and copies ran while one was open for 13% -> 5% of each run, Pallas kernels for 0% -> 6%
where the time goes in v1:
time: 382 us; the launch traced here: 376 us
  waiting for transfers between devices  159 us (42%)
  starting transfers between devices  58.7 us (15%)
  blocking collectives  52 us (14%)
  local copies, waits for them, and re-layouts  40.8 us (11%)
  Pallas kernels  32 us (8%)
  between operations  14.6 us (4%)
  other arithmetic  13.2 us (3%)
  matrix products  6.27 us (2%)
    all_gather x1, waiting for transfers between devices, on_device(): filled = lax.all_gather(mine, DP, axis=0, tiled=True)  85.9 us
    all_to_all x2, waiting for transfers between devices, layer_sum(): got = lax.all_to_all(part, RANKS, 0, 0)  39.5 us
    pallas_call x14, Pallas kernels, call(): pl.pallas_call(kernel, out_shape=out_shape, in_specs=[SMEM] * scalars + [...  32 us
    all_gather x3, blocking collectives, summed_over(): part = jnp.sum(lax.all_gather(part, axis), axis=0)  30.7 us
    unnamed x56, local copies, waits for them, and re-layouts  30.5 us
    ppermute x10, starting transfers between devices, on_device(): incoming = lax.ppermute(result, 's', pairs)  25.6 us
    all_to_all x2, waiting for transfers between devices, layer_sum(): mixed = lax.all_to_all(jnp.concatenate([dy, both], axis=2), QUARTERS, 0, 0)  16.8 us
    ppermute x10, waiting for transfers between devices, on_device(): incoming = lax.ppermute(result, 's', pairs)  16.5 us
  transfers between devices with their start and end apart: 16, of which 13 were waited for; matrix products, arithmetic and copies ran while one was open for 5% of the time, Pallas kernels for 6%

profile of v1, /device:TPU:1, one launch (start us, length us, event | category | flops | bytes accessed | tf_op | source)
XLA Modules:
  0.0 376.1 jit_solution(975880970000565928)
XLA Ops:
  12.7 85.9 %all-gather.10.cloned.1.call-done = bf16[4096,1024]{1,0:T(8,128)(2,1)} async-done(((bf16[64,1024]{1,0:T(8,128)(2,1)}), bf16[4096,1024]{1,0:T(8,128)(2,1)}) %all-gather.10.cloned.1.call-update) | async-done | bytes 8388624 | tf_op jit(solution)/shard_map/all_gather | solution.py:132
  98.8 3.4 copy-done.1
  115.2 3.5 collective-permute-start.1
  132.1 3.4 copy-done.4
  143.7 3.4 copy-done.5
  153.3 9.0 %all-to-all-start.1 = ((bf16[4,2,64,1024]{3,2,1,0:T(8,128)(2,1)}), bf16[4,2,64,1024]{3,2,1,0:T(8,128)(2,1)}, u32[]{:S(2)}, u32[]{:S(2)}) async-start(bf16[4,2,64,1024]{3,2,1,0:T(8,128)(2,1)} %copy.26), calls=%async_computation.1 | async-start | bytes 2097152 | tf_op jit(solution)/shard_map/all_to_all | solution.py:153
  162.4 3.4 copy-done.6
  169.9 3.9 %collective-permute-done.5.refs_0_ = bf16[16,4096]{1,0:T(8,128)(2,1)} collective-permute-done((bf16[16,4096]{1,0:T(8,128)(2,1)}, bf16[16,4096]{1,0:T(8,128)(2,1)}, u32[]{:S(2)}, u32[]{:S(2)}) %collective-permute-start.5) | collective-permute-done | bytes 131104 | tf_op jit(solution)/shard_map/ppermute | solution.py:224
  173.8 3.4 copy-done.7
  184.7 3.4 copy-done.8
  196.7 3.4 copy-done.9
  220.7 8.2 %all-to-all-start.3 = ((bf16[4,64,1536]{2,1,0:T(8,128)(2,1)}), bf16[4,64,1536]{2,1,0:T(8,128)(2,1)S(1)}, u32[]{:S(2)}, u32[]{:S(2)}) async-start(bf16[4,64,1536]{2,1,0:T(8,128)(2,1)} %pad_maximum_fusion.1), calls=%async_computation.3 | async-start | bytes 1572864 | tf_op jit(solution)/shard_map/all_to_all | solution.py:199
  231.0 8.7 %all-to-all-done.3 = bf16[4,64,1536]{2,1,0:T(8,128)(2,1)S(1)} async-done(((bf16[4,64,1536]{2,1,0:T(8,128)(2,1)}), bf16[4,64,1536]{2,1,0:T(8,128)(2,1)S(1)}, u32[]{:S(2)}, u32[]{:S(2)}) %all-to-all-start.3) | async-done | bytes 786464 | tf_op jit(solution)/shard_map/all_to_all | solution.py:199
  239.7 4.3 %all-to-all-start = ((bf16[4,64,1536]{2,1,0:T(8,128)(2,1)}), bf16[4,64,1536]{2,1,0:T(8,128)(2,1)S(1)}, u32[]{:S(2)}, u32[]{:S(2)}) async-start(bf16[4,64,1536]{2,1,0:T(8,128)(2,1)} %pad_maximum_fusion), calls=%async_computation | async-start | bytes 1572864 | tf_op jit(solution)/shard_map/all_to_all | solution.py:199
  246.8 8.1 %all-to-all-done = bf16[4,64,1536]{2,1,0:T(8,128)(2,1)S(1)} async-done(((bf16[4,64,1536]{2,1,0:T(8,128)(2,1)}), bf16[4,64,1536]{2,1,0:T(8,128)(2,1)S(1)}, u32[]{:S(2)}, u32[]{:S(2)}) %all-to-all-start) | async-done | bytes 786464 | tf_op jit(solution)/shard_map/all_to_all | solution.py:199
  254.9 5.0 %all-to-all-start.4 = ((bf16[16,32,1024]{2,1,0:T(8,128)(2,1)}), bf16[16,32,1024]{2,1,0:T(8,128)(2,1)}, u32[]{:S(2)}, u32[]{:S(2)}) async-start(bf16[16,32,1024]{2,1,0:T(8,128)(2,1)} %shard_map.141), calls=%async_computation.4 | async-start | bytes 2097152 | tf_op jit(solution)/shard_map/all_to_all | solution.py:211
  261.3 25.9 %all-to-all-done.4 = bf16[16,32,1024]{2,1,0:T(8,128)(2,1)} async-done(((bf16[16,32,1024]{2,1,0:T(8,128)(2,1)}), bf16[16,32,1024]{2,1,0:T(8,128)(2,1)}, u32[]{:S(2)}, u32[]{:S(2)}) %all-to-all-start.4) | async-done | bytes 1048608 | tf_op jit(solution)/shard_map/all_to_all | solution.py:211
  287.2 6.4 %all-to-all-start.2 = ((bf16[16,32,1024]{2,1,0:T(8,128)(2,1)}), bf16[16,32,1024]{2,1,0:T(8,128)(2,1)}, u32[]{:S(2)}, u32[]{:S(2)}) async-start(bf16[16,32,1024]{2,1,0:T(8,128)(2,1)} %shard_map.140), calls=%async_computation.2 | async-start | bytes 2097152 | tf_op jit(solution)/shard_map/all_to_all | solution.py:211
  293.7 10.1 %all-gather = f32[8,1,8,256]{3,2,1,0:T(8,128)S(1)} all-gather(f32[2,1,8,256]{3,2,1,0:T(8,128)S(1)} %copy-done.21), channel_id=2, replica_groups=mesh['s'=4,'x'=4,'zh'=4,'zl'=2,'c'=2] {'s'}, dimensions={0}, use_global_device_ids=true | all-gather | bytes 81920 | tf_op jit(solution)/shard_map/all_gather | solution.py:135
  307.2 13.6 %all-to-all-done.2 = bf16[16,32,1024]{2,1,0:T(8,128)(2,1)} async-done(((bf16[16,32,1024]{2,1,0:T(8,128)(2,1)}), bf16[16,32,1024]{2,1,0:T(8,128)(2,1)}, u32[]{:S(2)}, u32[]{:S(2)}) %all-to-all-start.2) | async-done | bytes 1048608 | tf_op jit(solution)/shard_map/all_to_all | solution.py:211
  322.2 11.2 %all-gather.1 = bf16[8,32,1024]{2,1,0:T(8,128)(2,1)S(1)} all-gather(bf16[2,32,1024]{2,1,0:T(8,128)(2,1)S(1)} %pad_maximum_fusion.5), channel_id=3, replica_groups=mesh['s'=4,'x'=4,'zh'=4,'zl'=2,'c'=2] {'s'}, dimensions={0}, use_global_device_ids=true | all-gather | bytes 655360 | tf_op jit(solution)/shard_map/all_gather | solution.py:238
  337.4 10.8 %all-gather.5 = f32[4,18,256]{2,1,0:T(8,128)S(1)} all-gather(f32[1,18,256]{2,1,0:T(8,128)S(1)} %maximum_bitcast_fusion.1), channel_id=4, replica_groups=mesh['s'=4,'x'=4,'zh'=4,'zl'=2,'c'=2] {'zl','c'}, dimensions={0}, use_global_device_ids=true | all-gather | bytes 92160 | tf_op jit(solution)/shard_map/all_gather | solution.py:106
  348.2 9.0 %all-gather.6 = f32[4,18,256]{2,1,0:T(8,128)S(1)} all-gather(f32[1,18,256]{2,1,0:T(8,128)S(1)} %bitcast.182), channel_id=5, replica_groups=mesh['s'=4,'x'=4,'zh'=4,'zl'=2,'c'=2] {'x'}, dimensions={0}, use_global_device_ids=true | all-gather | bytes 92160 | tf_op jit(solution)/shard_map/all_gather | solution.py:106
  357.2 10.8 %all-gather.7 = f32[4,18,256]{2,1,0:T(8,128)S(1)} all-gather(f32[1,18,256]{2,1,0:T(8,128)S(1)} %bitcast.183), channel_id=6, replica_groups=mesh['s'=4,'x'=4,'zh'=4,'zl'=2,'c'=2] {'zh'}, dimensions={0}, use_global_device_ids=true | all-gather | bytes 92160 | tf_op jit(solution)/shard_map/all_gather | solution.py:106
  (158 shorter events, 103.3 us)
Async XLA Ops:
  7.2 91.4 %all-gather.10.cloned.1.call-start = ((), (), s32[]{:S(2)}) async-start(), calls=%async_computation.5 | async-start | bytes 8519680 | tf_op jit(solution)/shard_map/all_gather | solution.py:132
  12.2 86.6 %copy-start.25 = (s32[256]{0:T(256)}, s32[256]{0:T(256)S(1)}, u32[]{:S(2)}) copy-start(s32[256]{0:T(256)S(1)} %and_select_fusion) | copy-start | bytes 3076
  104.4 5.2 %collective-permute-start = (bf16[16,4096]{1,0:T(8,128)(2,1)S(1)}, bf16[16,4096]{1,0:T(8,128)(2,1)S(1)}, u32[]{:S(2)}, u32[]{:S(2)}) collective-permute-start(bf16[16,4096]{1,0:T(8,128)(2,1)S(1)} %get-tuple-element.27), channel_id=1, source_target_pairs={{0,192},{64,0},{128,64},{192,128},{1,193},{65,1},{129,65},{193,129... | collective-permute-start | bytes 393224 | tf_op jit(solution)/shard_map/ppermute | solution.py:224
  115.2 5.4 %collective-permute-start.1 = (bf16[16,4096]{1,0:T(8,128)(2,1)S(1)}, bf16[16,4096]{1,0:T(8,128)(2,1)S(1)}, u32[]{:S(2)}, u32[]{:S(2)}) collective-permute-start(bf16[16,4096]{1,0:T(8,128)(2,1)S(1)} %get-tuple-element.28), channel_id=1, source_target_pairs={{0,192},{64,0},{128,64},{192,128},{1,193},{65,1},{129,65},{193,129... | collective-permute-start | bytes 393224 | tf_op jit(solution)/shard_map/ppermute | solution.py:224
  126.3 5.1 %collective-permute-start.2 = (bf16[16,4096]{1,0:T(8,128)(2,1)S(1)}, bf16[16,4096]{1,0:T(8,128)(2,1)S(1)}, u32[]{:S(2)}, u32[]{:S(2)}) collective-permute-start(bf16[16,4096]{1,0:T(8,128)(2,1)S(1)} %get-tuple-element.29), channel_id=1, source_target_pairs={{0,192},{64,0},{128,64},{192,128},{1,193},{65,1},{129,65},{193,129... | collective-permute-start | bytes 393224 | tf_op jit(solution)/shard_map/ppermute | solution.py:224
  137.7 6.0 %collective-permute-start.3 = (bf16[16,4096]{1,0:T(8,128)(2,1)S(1)}, bf16[16,4096]{1,0:T(8,128)(2,1)S(1)}, u32[]{:S(2)}, u32[]{:S(2)}) collective-permute-start(bf16[16,4096]{1,0:T(8,128)(2,1)S(1)} %get-tuple-element.30), channel_id=1, source_target_pairs={{0,192},{64,0},{128,64},{192,128},{1,193},{65,1},{129,65},{193,129... | collective-permute-start | bytes 393224 | tf_op jit(solution)/shard_map/ppermute | solution.py:224
  149.3 13.1 %collective-permute-start.4 = (bf16[16,4096]{1,0:T(8,128)(2,1)S(1)}, bf16[16,4096]{1,0:T(8,128)(2,1)S(1)}, u32[]{:S(2)}, u32[]{:S(2)}) collective-permute-start(bf16[16,4096]{1,0:T(8,128)(2,1)S(1)} %get-tuple-element.31), channel_id=1, source_target_pairs={{0,192},{64,0},{128,64},{192,128},{1,193},{65,1},{129,65},{193,129... | collective-permute-start | bytes 393224 | tf_op jit(solution)/shard_map/ppermute | solution.py:224
  153.3 67.4 %all-to-all-start.1 = ((bf16[4,2,64,1024]{3,2,1,0:T(8,128)(2,1)}), bf16[4,2,64,1024]{3,2,1,0:T(8,128)(2,1)}, u32[]{:S(2)}, u32[]{:S(2)}) async-start(bf16[4,2,64,1024]{3,2,1,0:T(8,128)(2,1)} %copy.26), calls=%async_computation.1 | async-start | bytes 2097152 | tf_op jit(solution)/shard_map/all_to_all | solution.py:153
  168.7 5.2 %collective-permute-start.5 = (bf16[16,4096]{1,0:T(8,128)(2,1)}, bf16[16,4096]{1,0:T(8,128)(2,1)}, u32[]{:S(2)}, u32[]{:S(2)}) collective-permute-start(bf16[16,4096]{1,0:T(8,128)(2,1)} %get-tuple-element.32), channel_id=1, source_target_pairs={{0,192},{64,0},{128,64},{192,128},{1,193},{65,1},{129,65},{193,129... | collective-permute-start | bytes 393224 | tf_op jit(solution)/shard_map/ppermute | solution.py:224
  180.5 4.1 %collective-permute-start.6 = (bf16[16,4096]{1,0:T(8,128)(2,1)}, bf16[16,4096]{1,0:T(8,128)(2,1)}, u32[]{:S(2)}, u32[]{:S(2)}) collective-permute-start(bf16[16,4096]{1,0:T(8,128)(2,1)} %get-tuple-element.33), channel_id=1, source_target_pairs={{0,192},{64,0},{128,64},{192,128},{1,193},{65,1},{129,65},{193,129... | collective-permute-start | bytes 393224 | tf_op jit(solution)/shard_map/ppermute | solution.py:224
  191.3 5.4 %collective-permute-start.7 = (bf16[16,4096]{1,0:T(8,128)(2,1)}, bf16[16,4096]{1,0:T(8,128)(2,1)}, u32[]{:S(2)}, u32[]{:S(2)}) collective-permute-start(bf16[16,4096]{1,0:T(8,128)(2,1)} %get-tuple-element.34), channel_id=1, source_target_pairs={{0,192},{64,0},{128,64},{192,128},{1,193},{65,1},{129,65},{193,129... | collective-permute-start | bytes 393224 | tf_op jit(solution)/shard_map/ppermute | solution.py:224
  200.1 6.0 %copy-start.12 = (f32[2,64,256]{2,1,0:T(8,128)S(1)}, f32[2,64,256]{2,1,0:T(8,128)}, u32[]{:S(2)}) copy-start(f32[2,64,256]{2,1,0:T(8,128)} %add_select_fusion.weights_ref) | copy-start | bytes 393220
  202.9 5.1 %collective-permute-start.8 = (bf16[16,4096]{1,0:T(8,128)(2,1)S(1)}, bf16[16,4096]{1,0:T(8,128)(2,1)S(1)}, u32[]{:S(2)}, u32[]{:S(2)}) collective-permute-start(bf16[16,4096]{1,0:T(8,128)(2,1)S(1)} %get-tuple-element.35), channel_id=1, source_target_pairs={{0,192},{64,0},{128,64},{192,128},{1,193},{65,1},{129,65},{193,129... | collective-permute-start | bytes 393224 | tf_op jit(solution)/shard_map/ppermute | solution.py:224
  210.2 6.3 %copy-start.20 = (bf16[16,4096]{1,0:T(8,128)(2,1)S(1)}, bf16[16,4096]{1,0:T(8,128)(2,1)}, u32[]{:S(2)}) copy-start(bf16[16,4096]{1,0:T(8,128)(2,1)} %get-tuple-element.55) | copy-start | bytes 393220
  210.2 5.1 %collective-permute-start.9 = (bf16[16,4096]{1,0:T(8,128)(2,1)S(1)}, bf16[16,4096]{1,0:T(8,128)(2,1)S(1)}, u32[]{:S(2)}, u32[]{:S(2)}) collective-permute-start(bf16[16,4096]{1,0:T(8,128)(2,1)S(1)} %get-tuple-element.36), channel_id=1, source_target_pairs={{0,192},{64,0},{128,64},{192,128},{1,193},{65,1},{129,65},{193,129... | collective-permute-start | bytes 393224 | tf_op jit(solution)/shard_map/ppermute | solution.py:224
  220.7 19.0 %all-to-all-start.3 = ((bf16[4,64,1536]{2,1,0:T(8,128)(2,1)}), bf16[4,64,1536]{2,1,0:T(8,128)(2,1)S(1)}, u32[]{:S(2)}, u32[]{:S(2)}) async-start(bf16[4,64,1536]{2,1,0:T(8,128)(2,1)} %pad_maximum_fusion.1), calls=%async_computation.3 | async-start | bytes 1572864 | tf_op jit(solution)/shard_map/all_to_all | solution.py:199
  239.7 15.1 %all-to-all-start = ((bf16[4,64,1536]{2,1,0:T(8,128)(2,1)}), bf16[4,64,1536]{2,1,0:T(8,128)(2,1)S(1)}, u32[]{:S(2)}, u32[]{:S(2)}) async-start(bf16[4,64,1536]{2,1,0:T(8,128)(2,1)} %pad_maximum_fusion), calls=%async_computation | async-start | bytes 1572864 | tf_op jit(solution)/shard_map/all_to_all | solution.py:199
  254.9 32.4 %all-to-all-start.4 = ((bf16[16,32,1024]{2,1,0:T(8,128)(2,1)}), bf16[16,32,1024]{2,1,0:T(8,128)(2,1)}, u32[]{:S(2)}, u32[]{:S(2)}) async-start(bf16[16,32,1024]{2,1,0:T(8,128)(2,1)} %shard_map.141), calls=%async_computation.4 | async-start | bytes 2097152 | tf_op jit(solution)/shard_map/all_to_all | solution.py:211
  259.8 33.8 %copy-start.21 = (f32[2,1,8,256]{3,2,1,0:T(8,128)S(1)}, f32[2,1,8,256]{3,2,1,0:T(8,128)}, u32[]{:S(2)}) copy-start(f32[2,1,8,256]{3,2,1,0:T(8,128)} %param.15) | copy-start | bytes 49156
  259.8 43.9 %copy-start.14 = (bf16[16,4096]{1,0:T(8,128)(2,1)S(1)}, bf16[16,4096]{1,0:T(8,128)(2,1)}, u32[]{:S(2)}) copy-start(bf16[16,4096]{1,0:T(8,128)(2,1)} %copy-done.13) | copy-start | bytes 393220
  259.8 43.9 %copy-start.16 = (bf16[16,4096]{1,0:T(8,128)(2,1)S(1)}, bf16[16,4096]{1,0:T(8,128)(2,1)}, u32[]{:S(2)}) copy-start(bf16[16,4096]{1,0:T(8,128)(2,1)} %copy-done.15) | copy-start | bytes 393220
  287.2 33.5 %all-to-all-start.2 = ((bf16[16,32,1024]{2,1,0:T(8,128)(2,1)}), bf16[16,32,1024]{2,1,0:T(8,128)(2,1)}, u32[]{:S(2)}, u32[]{:S(2)}) async-start(bf16[16,32,1024]{2,1,0:T(8,128)(2,1)} %shard_map.140), calls=%async_computation.2 | async-start | bytes 2097152 | tf_op jit(solution)/shard_map/all_to_all | solution.py:211
  307.2 26.6 %copy-start.18 = (bf16[256,1024]{1,0:T(8,128)(2,1)S(1)}, bf16[256,1024]{1,0:T(8,128)(2,1)}, u32[]{:S(2)}) copy-start(bf16[256,1024]{1,0:T(8,128)(2,1)} %param.17) | copy-start | bytes 1572868
  322.2 12.0 %copy-start.22 = (f32[2,256]{1,0:T(2,128)S(1)}, f32[2,256]{1,0:T(2,128)}, u32[]{:S(2)}) copy-start(f32[2,256]{1,0:T(2,128)} %param.14) | copy-start | bytes 6148
  (20 other events, 82.7 us)
Sparse Core Ops, SparseCore 0:
  11.4 87.1 all-gather.9
